TPU v7x, 256 devices: a whole 4x4x8 slice. The times are simulated.
256 devices in a mesh: seq: 64 (over z, y, core), fsdp: 4 (over x).
Axes of the slice: x: 4, y: 4, z: 8, core: 2. Of those that a mesh axis runs over, the one named last changes fastest.
Arguments:
- inputs: bfloat16 [4, 8192, 3584], P('fsdp', 'seq'), may hold values from -36 to 36
- keys_queries: bfloat16 [4, 8192, 256], P('fsdp', 'seq'), may hold values from -0.29882812 to 0.29882812
- log_decay: float32 [4, 56, 8192], P('fsdp', None, 'seq'), may hold values from -1.5 to 0, as said below
- skip: float32 [56], replicated, may hold values from 0.5 to 1.5
- classifier: bfloat16 [3584, 128], P('fsdp'), may hold values from -0.09375 to 0.09375
Outputs:
- mixed: bfloat16 [4, 8192, 3584], P('fsdp', 'seq')
- logits: float32 [4, 128], P('fsdp')
Inputs may be any that keep to these rules, and one draw needn't show every extreme that they name: `log_decay`: log-decays are negative.
All inputs are finite; a program needn't handle non-finite values.
Results may differ from a plain program's by a relative error of at most 0.0051.
Values may be sent and summed in bfloat16 or wider, within the bound.
A program may use at most 256 MiB of HBM per device.

v0:
```python
import jax
import jax.numpy as jnp
from jax import lax
from jax.sharding import PartitionSpec as P

N = 128
GROUP = 128
epsilon = 1e-06


def linker(earlier, latter):
    return (earlier[0] + latter[0], jnp.exp(latter[0]) * earlier[1] + latter[1])


def local(inputs, keys_queries, log_decay, skip, classifier):
    copies, positions, channels = inputs.shape
    head_count = log_decay.shape[1]
    head_dim = channels // head_count
    blocks = positions // GROUP
    key_rows = keys_queries[:, :, :N].reshape(copies, blocks, GROUP, N)
    queries = keys_queries[:, :, N:].reshape(copies, blocks, GROUP, N)
    values = inputs.reshape(copies, blocks, GROUP, head_count, head_dim)
    cumulative = jnp.cumsum(log_decay.reshape(copies, head_count, blocks, GROUP), axis=-1)
    block_decay = cumulative[..., -1]
    weighted = (key_rows[:, None] * jnp.exp(block_decay[..., None] - cumulative)[..., None]).astype(
        jnp.bfloat16
    )
    block_state = jnp.einsum(
        "chkun,ckuhp->kchnp", weighted, values, preferred_element_type=jnp.float32
    )

    def advance(running, member):
        return (jnp.exp(member[0])[..., None, None] * running + member[1], running)

    device_state, starts = lax.scan(
        advance, jnp.zeros_like(block_state[0]), (jnp.moveaxis(block_decay, 2, 0), block_state)
    )
    device_decay = jnp.sum(block_decay, axis=-1)
    axis_count = lax.axis_size("seq")
    flattened = device_state.reshape(copies, head_count, 1, N * head_dim)
    decay_copies = jnp.broadcast_to(
        device_decay[:, :, None, None], (copies, head_count, 1, axis_count)
    )
    totals = lax.associative_scan(
        linker,
        (
            lax.all_to_all(decay_copies, "seq", split_axis=3, concat_axis=2, tiled=True),
            lax.all_to_all(flattened, "seq", split_axis=3, concat_axis=2, tiled=True),
        ),
        axis=2,
    )[1]
    shifted = jnp.concatenate([jnp.zeros_like(totals[:, :, :1]), totals[:, :, :-1]], axis=2)
    incoming = lax.all_to_all(shifted, "seq", split_axis=2, concat_axis=3, tiled=True)
    incoming = incoming.reshape(copies, head_count, N, head_dim)
    preceding = jnp.moveaxis(jnp.cumsum(block_decay, axis=-1) - block_decay, 2, 0)
    carried = (jnp.exp(preceding)[..., None, None] * incoming[None] + starts).astype(jnp.bfloat16)
    growth = jnp.exp(cumulative).transpose(0, 2, 3, 1)[..., None]
    carried_out = (
        jnp.einsum("ckqn,kchnp->ckqhp", queries, carried, preferred_element_type=jnp.float32)
        * growth
    )
    causal = jnp.arange(GROUP)[:, None] >= jnp.arange(GROUP)[None, :]
    scores = jnp.einsum("cktn,ckun->cktu", queries, key_rows, preferred_element_type=jnp.float32)
    decay_gap = jnp.where(causal, cumulative[..., :, None] - cumulative[..., None, :], -jnp.inf)
    mixing = (scores[:, None] * jnp.exp(decay_gap)).astype(jnp.bfloat16)
    diagonal = jnp.einsum("chktu,ckuhp->ckthp", mixing, values, preferred_element_type=jnp.float32)
    mixed_full = diagonal + carried_out + skip[:, None] * values.astype(jnp.float32)
    mixed = mixed_full.astype(jnp.bfloat16).reshape(copies, positions, channels)
    partial_sum = jnp.sum(mixed_full, axis=(1, 2)).reshape(copies, channels)
    pooled = lax.psum(partial_sum, "seq") / (positions * lax.axis_size("seq"))
    normed = (
        pooled / jnp.sqrt(jnp.mean(pooled * pooled, axis=-1, keepdims=True) + epsilon)
    ).astype(jnp.bfloat16)
    logits = jnp.dot(
        normed,
        lax.all_gather(classifier, "fsdp", axis=0, tiled=True),
        preferred_element_type=jnp.float32,
    )
    return (mixed, logits)


def solution(mesh):
    return jax.shard_map(
        local,
        mesh=mesh,
        in_specs=(
            P("fsdp", "seq", None),
            P("fsdp", "seq", None),
            P("fsdp", None, "seq"),
            P(),
            P("fsdp", None),
        ),
        out_specs=(P("fsdp", "seq", None), P("fsdp", None)),
        check_vma=False,
    )
```

profile of v0, /device:TPU:2, one launch (start us, length us, event | category | flops | bytes accessed | tf_op | source)
XLA Modules:
  0.0 497.6 jit_solution(18033312582586399048)
XLA Ops:
  0.6 1.1 reduce_window_sum.17
  2.5 12.1 %all-to-all-start.1 = ((f32[1,56,1,64]{1,2,0,3:T(1,128)}), f32[1,56,1,64]{1,2,0,3:T(1,128)S(1)}, u32[]{:S(2)}, u32[]{:S(2)}) async-start(f32[1,56,1,64]{1,2,0,3:T(1,128)} %broadcast_in_dim.18), calls=%async_computation.1 | async-start | bytes 65536 | tf_op jit(solution)/shard_map/all_to_all | solution.py:47
  14.7 1.6 copy.45
  16.3 1.3 fusion.10
  17.6 4.5 copy.57
  22.6 38.4 %reduce.6 = f32[8192,56]{1,0:T(8,128)} reduce(f32[8192,1,1,56]{3,2,1,0:T(1,128)} %bitcast.76, f32[]{:T(128)} %broadcast.116), dimensions={1,2}, to_apply=%bitcast.65.reduce_sub_computation | reduce | bytes 3670020
  61.0 6.9 %reshape.245 = f32[64,1,7168]{2,1,0:T(1,128)} reshape(f32[8192,56]{1,0:T(8,128)} %reduce.6) | data formatting | bytes 3670016
  67.9 10.5 %all-to-all-start = ((f32[64,1,7168]{2,1,0:T(1,128)}), f32[64,1,7168]{2,1,0:T(1,128)S(1)}, u32[]{:S(2)}, u32[]{:S(2)}) async-start(f32[64,1,7168]{2,1,0:T(1,128)} %reshape.245), calls=%async_computation | async-start | bytes 3670016 | tf_op jit(solution)/shard_map/all_to_all | solution.py:48
  78.8 45.2 %all-to-all-done = f32[64,1,7168]{2,1,0:T(1,128)S(1)} async-done(((f32[64,1,7168]{2,1,0:T(1,128)}), f32[64,1,7168]{2,1,0:T(1,128)S(1)}, u32[]{:S(2)}, u32[]{:S(2)}) %all-to-all-start) | async-done | bytes 1835040 | tf_op jit(solution)/shard_map/all_to_all | solution.py:48
  124.0 6.8 %reduce.7 = f32[64,7168]{1,0:T(8,128)} reduce(f32[64,1,7168]{2,1,0:T(1,128)S(1)} %all-to-all-done, f32[]{:T(128)} %broadcast.116), dimensions={1}, to_apply=%all_to_all.10.reduce_sub_computation | reduce | bytes 3670020 | tf_op jit(solution)/shard_map/all_to_all | solution.py:48
  130.7 11.1 %reshape.246 = f32[8192,1,1,56]{3,2,1,0:T(1,128)} reshape(f32[64,7168]{1,0:T(8,128)} %reduce.7) | data formatting | bytes 3670016
  141.8 4.1 fusion.34
  145.9 1.5 slice.192
  148.0 2.2 copy.60
  150.2 1.5 copy.61
  151.7 1.5 multiply_add_fusion
  156.4 1.0 add.138
  157.4 16.4 %pad.85 = f32[1,56,64,128]{3,1,0,2:T(8,128)} pad(f32[1,56,32,128]{3,1,0,2:T(8,128)} %add.138, f32[]{:T(128)} %constant.16.clone.1), padding=0_0_0x0_0_0x1_0_1x0_0_0 | pad | bytes 2752516
  173.8 1.5 copy.62
  175.4 1.8 fusion.11
  177.2 11.0 %pad.61 = f32[1,56,63,128]{3,1,0,2:T(8,128)} pad(f32[1,56,32,128]{3,1,0,2:T(8,128)S(1)} %pad_maximum_fusion, f32[]{:T(128)} %constant.16.clone.1), padding=0_0_0x0_0_0x0_0_1x0_0_0 | pad | bytes 2723844 | tf_op jit(solution)/shard_map/slice | solution.py:52
  188.3 1.7 slice_add_fusion.5
  190.0 1.3 concatenate.23
  191.3 5.3 %all-to-all-start.2 = ((f32[1,56,64,128]{3,1,0,2:T(8,128)}), f32[1,56,64,128]{3,1,0,2:T(8,128)S(1)}, u32[]{:S(2)}, u32[]{:S(2)}) async-start(f32[1,56,64,128]{3,1,0,2:T(8,128)} %concatenate.23), calls=%async_computation.2 | async-start | bytes 3670016 | tf_op jit(solution)/shard_map/all_to_all | solution.py:53
  196.6 2.6 copy.54
  199.4 2.6 fusion
  202.0 15.5 %all_gather.3 = bf16[3584,128]{1,0:T(8,128)(2,1)} all-gather(bf16[896,128]{1,0:T(8,128)(2,1)S(1)} %copy-done.10), channel_id=1, replica_groups=mesh['seq'=64,'fsdp'=4] {'fsdp'}, dimensions={0}, use_global_device_ids=true | all-gather | bytes 1146880 | tf_op jit(solution)/shard_map/all_gather | solution.py:76
  217.5 24.9 %all-to-all-done.2 = f32[1,56,64,128]{3,1,0,2:T(8,128)S(1)} async-done(((f32[1,56,64,128]{3,1,0,2:T(8,128)}), f32[1,56,64,128]{3,1,0,2:T(8,128)S(1)}, u32[]{:S(2)}, u32[]{:S(2)}) %all-to-all-start.2) | async-done | bytes 1835040 | tf_op jit(solution)/shard_map/all_to_all | solution.py:53
  242.8 1.7 convert_element_type.57
  244.6 3.3 fusion.35
  248.0 246.3 %psum.7 = f32[1,3584]{1,0:T(1,128)S(1)} all-reduce(f32[1,3584]{1,0:T(1,128)S(1)} %reshape.236), channel_id=1, replica_groups=mesh['seq'=64,'fsdp'=4] {'seq'}, use_global_device_ids=true, to_apply=%region_2.3 | all-reduce | flops 3584 | bytes 28672 | tf_op jit(solution)/shard_map/psum | solution.py:70
  495.6 1.3 copy.55
  (95 shorter events, 7.6 us)
Async XLA Ops:
  0.6 15.7 %copy-start.8 = (bf16[1,128,256]{2,1,0:T(8,128)(2,1)S(1)}, bf16[1,128,256]{2,1,0:T(8,128)(2,1)}, u32[]{:S(2)}) copy-start(bf16[1,128,256]{2,1,0:T(8,128)(2,1)} %param.6) | copy-start | bytes 196612
  2.5 65.4 %all-to-all-start.1 = ((f32[1,56,1,64]{1,2,0,3:T(1,128)}), f32[1,56,1,64]{1,2,0,3:T(1,128)S(1)}, u32[]{:S(2)}, u32[]{:S(2)}) async-start(f32[1,56,1,64]{1,2,0,3:T(1,128)} %broadcast_in_dim.18), calls=%async_computation.1 | async-start | bytes 65536 | tf_op jit(solution)/shard_map/all_to_all | solution.py:47
  16.3 5.8 %copy-start.5 = (bf16[1,128,3584]{1,2,0:T(8,128)(2,1)}, bf16[1,128,3584]{1,2,0:T(8,128)(2,1)S(1)}, u32[]{:S(2)}) copy-start(bf16[1,128,3584]{1,2,0:T(8,128)(2,1)S(1)} %copy.45) | copy-start | bytes 2752516
  67.9 56.0 %all-to-all-start = ((f32[64,1,7168]{2,1,0:T(1,128)}), f32[64,1,7168]{2,1,0:T(1,128)S(1)}, u32[]{:S(2)}, u32[]{:S(2)}) async-start(f32[64,1,7168]{2,1,0:T(1,128)} %reshape.245), calls=%async_computation | async-start | bytes 3670016 | tf_op jit(solution)/shard_map/all_to_all | solution.py:48
  141.8 4.1 copy-start
  155.4 0.9 copy-start.2
  157.4 16.4 %copy-start.1 = (f32[1,56,31,128]{1,3,2,0:T(8,128)S(1)}, f32[1,56,31,128]{1,3,2,0:T(8,128)}, u32[]{:S(2)}) copy-start(f32[1,56,31,128]{1,3,2,0:T(8,128)} %slice.192) | copy-start | bytes 2666500
  173.8 1.5 copy-start.9
  177.2 11.1 %copy-start.4 = (f32[1,56,64,128]{3,1,0,2:T(8,128)S(1)}, f32[1,56,64,128]{3,1,0,2:T(8,128)}, u32[]{:S(2)}) copy-start(f32[1,56,64,128]{3,1,0,2:T(8,128)} %pad.85) | copy-start | bytes 5505028
  191.3 51.1 %all-to-all-start.2 = ((f32[1,56,64,128]{3,1,0,2:T(8,128)}), f32[1,56,64,128]{3,1,0,2:T(8,128)S(1)}, u32[]{:S(2)}, u32[]{:S(2)}) async-start(f32[1,56,64,128]{3,1,0,2:T(8,128)} %concatenate.23), calls=%async_computation.2 | async-start | bytes 3670016 | tf_op jit(solution)/shard_map/all_to_all | solution.py:53
  196.6 2.8 copy-start.6
  199.4 2.6 copy-start.10
  242.8 1.8 copy-start.3
  242.8 1.8 copy-start.11
  247.9 249.0 %copy-start.7 = (bf16[3584,128]{1,0:T(8,128)(2,1)S(1)}, bf16[3584,128]{1,0:T(8,128)(2,1)}, u32[]{:S(2)}) copy-start(bf16[3584,128]{1,0:T(8,128)(2,1)} %all_gather.3) | copy-start | bytes 2752516
where the time goes:
time: 500 us; the launch traced here: 498 us
  blocking collectives  262 us (52%)
  local copies, waits for them, and re-layouts  73.5 us (15%)
  waiting for transfers between devices  70.1 us (14%)
  other arithmetic  54.6 us (11%)
  starting transfers between devices  27.9 us (6%)
  matrix products  7.99 us (2%)
    psum x1, blocking collectives, local(): pooled = lax.psum(partial_sum, 'seq') / (positions * lax.axis_size('seq'))  246 us
    all_to_all x1, waiting for transfers between devices, local(): lax.all_to_all(flattened, 'seq', split_axis=3, concat_axis=2, tiled=True)  45.2 us
    unnamed x34, local copies, waits for them, and re-layouts  44 us
    unnamed x1, other arithmetic  38.4 us
    all_to_all x1, waiting for transfers between devices, local(): lax.all_to_all(shifted, 'seq', split_axis=2, concat_axis=3, tiled=True)  24.9 us
    all_gather x1, blocking collectives, local(): lax.all_gather(classifier, 'fsdp', axis=0, tiled=True)  15.5 us
    all_to_all x1, starting transfers between devices, local(): lax.all_to_all(decay_copies, 'seq', split_axis=3, concat_axis=2, tiled=True)  12.1 us
    slice x1, local copies, waits for them, and re-layouts, local(): totals[:, :, :-1]  11 us
  transfers between devices with their start and end apart: 3, of which 2 were waited for; matrix products, arithmetic and copies ran while one was open for 12% of the time, Pallas kernels for 0%

commit v1 on v0

--- a/solution.py
+++ b/solution.py
@@ -2,6 +2,7 @@
 import jax.numpy as jnp
 from jax import lax
 from jax.sharding import PartitionSpec as P
+from jax.lax import all_gather
 
 N = 128
 GROUP = 128
@@ -67,7 +68,9 @@
     mixed_full = diagonal + carried_out + skip[:, None] * values.astype(jnp.float32)
     mixed = mixed_full.astype(jnp.bfloat16).reshape(copies, positions, channels)
     partial_sum = jnp.sum(mixed_full, axis=(1, 2)).reshape(copies, channels)
-    pooled = lax.psum(partial_sum, "seq") / (positions * lax.axis_size("seq"))
+    pooled = jnp.sum(all_gather(partial_sum, axis_name="seq"), axis=0) / (
+        positions * lax.axis_size("seq")
+    )
     normed = (
         pooled / jnp.sqrt(jnp.mean(pooled * pooled, axis=-1, keepdims=True) + epsilon)
     ).astype(jnp.bfloat16)

time: 500 us -> 306 us (0.61)
  blocking collectives: 262 us -> 65.6 us
    psum x1 -> x0, blocking collectives: 246 us -> none  [local(): pooled = lax.psum(partial_sum, 'seq') / (positions * lax.axis_size('seq'))]
    all_gather x0 -> x1, blocking collectives: none -> 50.2 us  [local(): all_gather(partial_sum, axis_name='seq')]
  transfers between devices with their start and end apart: 3 -> 3, of which waited for: 2 -> 2; matrix products, arithmetic and copies ran while one was open for 12% -> 19% of each run, Pallas kernels for 0% -> 0%
where the time goes in v1:
time: 306 us; the launch traced here: 302 us
  local copies, waits for them, and re-layouts  73.5 us (24%)
  waiting for transfers between devices  70.1 us (23%)
  blocking collectives  65.6 us (21%)
  other arithmetic  55.1 us (18%)
  starting transfers between devices  27.9 us (9%)
  matrix products  7.99 us (3%)
    all_gather x1, blocking collectives, local(): all_gather(partial_sum, axis_name='seq')  50.2 us
    all_to_all x1, waiting for transfers between devices, local(): lax.all_to_all(flattened, 'seq', split_axis=3, concat_axis=2, tiled=True)  45.2 us
    unnamed x34, local copies, waits for them, and re-layouts  44 us
    unnamed x1, other arithmetic  38.4 us
    all_to_all x1, waiting for transfers between devices, local(): lax.all_to_all(shifted, 'seq', split_axis=2, concat_axis=3, tiled=True)  24.9 us
    all_gather x1, blocking collectives, local(): lax.all_gather(classifier, 'fsdp', axis=0, tiled=True)  15.5 us
    all_to_all x1, starting transfers between devices, local(): lax.all_to_all(decay_copies, 'seq', split_axis=3, concat_axis=2, tiled=True)  12.1 us
    slice x1, local copies, waits for them, and re-layouts, local(): totals[:, :, :-1]  11 us
  transfers between devices with their start and end apart: 3, of which 2 were waited for; matrix products, arithmetic and copies ran while one was open for 19% of the time, Pallas kernels for 0%

profile of v1, /device:TPU:2, one launch (start us, length us, event | category | flops | bytes accessed | tf_op | source)
XLA Modules:
  0.0 302.0 jit_solution(15744556721898108986)
XLA Ops:
  0.6 1.1 reduce_window_sum.17
  2.5 12.1 %all-to-all-start.1 = ((f32[1,56,1,64]{1,2,0,3:T(1,128)}), f32[1,56,1,64]{1,2,0,3:T(1,128)S(1)}, u32[]{:S(2)}, u32[]{:S(2)}) async-start(f32[1,56,1,64]{1,2,0,3:T(1,128)} %broadcast_in_dim.18), calls=%async_computation.1 | async-start | bytes 65536 | tf_op jit(solution)/shard_map/all_to_all | solution.py:48
  14.7 1.6 copy.34
  16.3 1.3 fusion.10
  17.6 4.5 %copy.46 = f32[56,128,64]{0,2,1:T(8,128)} copy(f32[56,128,64]{1,2,0:T(8,128)S(1)} %fusion.10) | data formatting | bytes 3670016 | tf_op jit(solution)/shard_map/reshape | solution.py:41
  22.6 38.4 %reduce.8 = f32[8192,56]{1,0:T(8,128)} reduce(f32[8192,1,1,56]{3,2,1,0:T(1,128)} %bitcast.74, f32[]{:T(128)} %broadcast.126), dimensions={1,2}, to_apply=%bitcast.62.reduce_sub_computation | reduce | bytes 3670020
  61.0 6.9 %reshape.248 = f32[64,1,7168]{2,1,0:T(1,128)} reshape(f32[8192,56]{1,0:T(8,128)} %reduce.8) | data formatting | bytes 3670016
  67.9 10.5 %all-to-all-start = ((f32[64,1,7168]{2,1,0:T(1,128)}), f32[64,1,7168]{2,1,0:T(1,128)S(1)}, u32[]{:S(2)}, u32[]{:S(2)}) async-start(f32[64,1,7168]{2,1,0:T(1,128)} %reshape.248), calls=%async_computation | async-start | bytes 3670016 | tf_op jit(solution)/shard_map/all_to_all | solution.py:49
  78.8 45.2 %all-to-all-done = f32[64,1,7168]{2,1,0:T(1,128)S(1)} async-done(((f32[64,1,7168]{2,1,0:T(1,128)}), f32[64,1,7168]{2,1,0:T(1,128)S(1)}, u32[]{:S(2)}, u32[]{:S(2)}) %all-to-all-start) | async-done | bytes 1835040 | tf_op jit(solution)/shard_map/all_to_all | solution.py:49
  124.0 6.8 %reduce.9 = f32[64,7168]{1,0:T(8,128)} reduce(f32[64,1,7168]{2,1,0:T(1,128)S(1)} %all-to-all-done, f32[]{:T(128)} %broadcast.126), dimensions={1}, to_apply=%all_to_all.10.reduce_sub_computation | reduce | bytes 3670020 | tf_op jit(solution)/shard_map/all_to_all | solution.py:49
  130.7 11.1 %reshape.249 = f32[8192,1,1,56]{3,2,1,0:T(1,128)} reshape(f32[64,7168]{1,0:T(8,128)} %reduce.9) | data formatting | bytes 3670016
  141.8 4.1 %fusion.26 = (f32[1,56,32,128]{1,3,2,0:T(8,128)}, f32[1,56,32,128]{1,3,2,0:T(8,128)S(1)}) fusion(f32[1,56,64,128]{1,3,2,0:T(8,128)} %bitcast.71), kind=kLoop, calls=%fused_computation.69 | loop fusion | bytes 3670016 | tf_op jit(solution)/shard_map/slice | solution.py:45
  145.9 1.5 slice.192
  148.0 2.2 copy.49
  150.2 1.5 copy.50
  151.7 1.5 multiply_add_fusion
  156.4 1.0 add.136
  157.4 16.4 %pad.85 = f32[1,56,64,128]{3,1,0,2:T(8,128)} pad(f32[1,56,32,128]{3,1,0,2:T(8,128)} %add.136, f32[]{:T(128)} %constant.16.clone.1), padding=0_0_0x0_0_0x1_0_1x0_0_0 | pad | bytes 2752516
  173.8 1.5 copy.51
  175.4 1.8 fusion.11
  177.2 11.0 %pad.61 = f32[1,56,63,128]{3,1,0,2:T(8,128)} pad(f32[1,56,32,128]{3,1,0,2:T(8,128)S(1)} %pad_maximum_fusion, f32[]{:T(128)} %constant.16.clone.1), padding=0_0_0x0_0_0x0_0_1x0_0_0 | pad | bytes 2723844 | tf_op jit(solution)/shard_map/slice | solution.py:53
  188.3 1.7 slice_add_fusion.5
  190.0 1.3 concatenate.23
  191.3 5.3 %all-to-all-start.2 = ((f32[1,56,64,128]{3,1,0,2:T(8,128)}), f32[1,56,64,128]{3,1,0,2:T(8,128)S(1)}, u32[]{:S(2)}, u32[]{:S(2)}) async-start(f32[1,56,64,128]{3,1,0,2:T(8,128)} %concatenate.23), calls=%async_computation.2 | async-start | bytes 3670016 | tf_op jit(solution)/shard_map/all_to_all | solution.py:54
  196.6 2.6 copy.43
  199.4 2.6 fusion
  202.0 15.5 %all_gather.7 = bf16[3584,128]{1,0:T(8,128)(2,1)} all-gather(bf16[896,128]{1,0:T(8,128)(2,1)S(1)} %copy-done.10), channel_id=1, replica_groups=mesh['seq'=64,'fsdp'=4] {'fsdp'}, dimensions={0}, use_global_device_ids=true | all-gather | bytes 1146880 | tf_op jit(solution)/shard_map/all_gather | solution.py:79
  217.5 24.9 %all-to-all-done.2 = f32[1,56,64,128]{3,1,0,2:T(8,128)S(1)} async-done(((f32[1,56,64,128]{3,1,0,2:T(8,128)}), f32[1,56,64,128]{3,1,0,2:T(8,128)S(1)}, u32[]{:S(2)}, u32[]{:S(2)}) %all-to-all-start.2) | async-done | bytes 1835040 | tf_op jit(solution)/shard_map/all_to_all | solution.py:54
  242.8 1.7 convert_element_type.60
  244.6 3.3 %fusion.27 = (f32[56,64]{1,0:T(8,128)S(1)}, bf16[1,1,128,56,64]{2,4,3,1,0:T(8,128)(2,1)S(1)}) fusion(f32[1,1,128,56,64]{2,4,3,1,0:T(8,128)S(1)} %bitcast.75, f32[56]{0:T(128)S(1)} %copy-done.11, f32[128,56]{0,1:T(8,128)S(1)} %exponential_bitcast_fusion, bf16[56,128,64]{2,1,0:T(8,128)(2,1)} %convert_element_type.60, bf16[1,128,256]{2,1,0:T(8,128)(2,1)S(1)} %copy-done.8, ...), kind=kOutput, calls=%fused_computation.70 | convolution fusion | flops 120189440 | bytes 5581312 | tf_op jit(solution)/shard_map/ckqn,kchnp->ckqhp/dot_general | solution.py:60
  248.0 50.2 %all_gather.6 = f32[64,1,3584]{2,1,0:T(1,128)S(1)} all-gather(f32[1,1,3584]{2,1,0:T(1,128)S(1)} %all_gather_reshape.3), channel_id=1, replica_groups=mesh['seq'=64,'fsdp'=4] {'seq'}, dimensions={0}, use_global_device_ids=true | all-gather | bytes 931840 | tf_op jit(solution)/shard_map/all_gather | solution.py:71
  300.0 1.3 copy.44
  (98 shorter events, 8.2 us)
Async XLA Ops:
  0.6 15.7 %copy-start.8 = (bf16[1,128,256]{2,1,0:T(8,128)(2,1)S(1)}, bf16[1,128,256]{2,1,0:T(8,128)(2,1)}, u32[]{:S(2)}) copy-start(bf16[1,128,256]{2,1,0:T(8,128)(2,1)} %param.6) | copy-start | bytes 196612
  2.5 65.4 %all-to-all-start.1 = ((f32[1,56,1,64]{1,2,0,3:T(1,128)}), f32[1,56,1,64]{1,2,0,3:T(1,128)S(1)}, u32[]{:S(2)}, u32[]{:S(2)}) async-start(f32[1,56,1,64]{1,2,0,3:T(1,128)} %broadcast_in_dim.18), calls=%async_computation.1 | async-start | bytes 65536 | tf_op jit(solution)/shard_map/all_to_all | solution.py:48
  16.3 5.8 %copy-start.5 = (bf16[1,128,3584]{1,2,0:T(8,128)(2,1)}, bf16[1,128,3584]{1,2,0:T(8,128)(2,1)S(1)}, u32[]{:S(2)}) copy-start(bf16[1,128,3584]{1,2,0:T(8,128)(2,1)S(1)} %copy.34) | copy-start | bytes 2752516
  67.9 56.0 %all-to-all-start = ((f32[64,1,7168]{2,1,0:T(1,128)}), f32[64,1,7168]{2,1,0:T(1,128)S(1)}, u32[]{:S(2)}, u32[]{:S(2)}) async-start(f32[64,1,7168]{2,1,0:T(1,128)} %reshape.248), calls=%async_computation | async-start | bytes 3670016 | tf_op jit(solution)/shard_map/all_to_all | solution.py:49
  141.8 4.1 %copy-start = (f32[8192,1,1,56]{3,2,1,0:T(1,128)S(1)}, f32[8192,1,1,56]{3,2,1,0:T(1,128)}, u32[]{:S(2)}) copy-start(f32[8192,1,1,56]{3,2,1,0:T(1,128)} %reshape.249) | copy-start | bytes 5505028
  155.4 0.9 copy-start.2
  157.4 16.4 %copy-start.1 = (f32[1,56,31,128]{1,3,2,0:T(8,128)S(1)}, f32[1,56,31,128]{1,3,2,0:T(8,128)}, u32[]{:S(2)}) copy-start(f32[1,56,31,128]{1,3,2,0:T(8,128)} %slice.192) | copy-start | bytes 2666500
  173.8 1.5 copy-start.9
  177.2 11.1 %copy-start.4 = (f32[1,56,64,128]{3,1,0,2:T(8,128)S(1)}, f32[1,56,64,128]{3,1,0,2:T(8,128)}, u32[]{:S(2)}) copy-start(f32[1,56,64,128]{3,1,0,2:T(8,128)} %pad.85) | copy-start | bytes 5505028
  191.3 51.1 %all-to-all-start.2 = ((f32[1,56,64,128]{3,1,0,2:T(8,128)}), f32[1,56,64,128]{3,1,0,2:T(8,128)S(1)}, u32[]{:S(2)}, u32[]{:S(2)}) async-start(f32[1,56,64,128]{3,1,0,2:T(8,128)} %concatenate.23), calls=%async_computation.2 | async-start | bytes 3670016 | tf_op jit(solution)/shard_map/all_to_all | solution.py:54
  196.6 2.8 copy-start.6
  199.4 2.6 copy-start.10
  242.8 1.8 copy-start.3
  242.8 1.8 copy-start.11
  248.0 53.3 %copy-start.7 = (bf16[3584,128]{1,0:T(8,128)(2,1)S(1)}, bf16[3584,128]{1,0:T(8,128)(2,1)}, u32[]{:S(2)}) copy-start(bf16[3584,128]{1,0:T(8,128)(2,1)} %all_gather.7) | copy-start | bytes 2752516
